TPU v7x, 32 devices: a whole 2x2x4 slice. The times are simulated.
32 devices in a mesh: grp: 2 (over y), ev: 2 (over x), loc: 8 (over z, core).
Axes of the slice: x: 2, y: 2, z: 4, core: 2. Of those that a mesh axis runs over, the one named last changes fastest.
Arguments:
- intensity_bin: int32 [256, 16384], P('ev', ('grp', 'loc')), parts along dimension 1, may hold values from 0 to 62
- bin_fraction: bfloat16 [256, 16384], P('ev', ('grp', 'loc')), parts along dimension 1, may hold values from 0 to 1
- footprint_mask: int32 [256, 128], P('ev', ('grp', 'loc')), parts along dimension 1, may hold values 0 or 1
- location_contract: int32 [16384], P(('grp', 'loc')), parts along dimension 0, may hold values from 0 to 2047
- location_class: int32 [16384], P(('grp', 'loc')), parts along dimension 0, may hold values from 0 to 127
- exposure: float32 [16384], P(('grp', 'loc')), parts along dimension 0, may hold values from 0.32 to 3.2
- curves: float32 [128, 64], replicated, may hold values from 0 to 1
- event_year: int32 [256], P('ev'), may hold values from 0 to 127
- occ_retention: float32 [4096], P('grp'), parts along dimension 0, may hold values from 0.2 to 0.8
- occ_limit: float32 [4096], P('grp'), parts along dimension 0, may hold values from 0.8 to 2.5
- agg_retention: float32 [4096], P('grp'), parts along dimension 0, may hold values from 0.125 to 0.375
- agg_limit: float32 [4096], P('grp'), parts along dimension 0, may hold values from 0.375 to 1
Outputs:
- annual: float32 [4096, 128], P(('grp', 'loc'), 'ev'), parts along dimension 0
- year_mean: float32 [256], P(('grp', 'ev')), parts along dimension 0
There are 2 independent parts, one for each index of `grp`. A program takes and returns all parts, laid end to end along the dimension named above; an argument that names none is the same for every part. Nothing has to cross between parts.
All inputs are finite; a program needn't handle non-finite values. No bound on the sum of `footprint_mask` on one device may be relied on, other than what follows from the above.
Results may differ from a plain program's by a relative error of at most 0.0016.
Values sent between devices are 32-bit elements; how exact they have to be, the bound alone decides.
No kernel may reach another device: no remote copies, remote signals or barrier semaphores. Data moves between devices by JAX's collectives and lax.ppermute only.
A program may use at most 64 MiB of HBM per device.

v0:
```python
import math

import jax
import jax.numpy as jnp
from jax import lax
from jax.sharding import PartitionSpec as P

YR_DEV = 64


def local(
    intensity_bin,
    bin_fraction,
    footprint_mask,
    location_contract,
    location_class,
    exposure,
    curves,
    event_year,
    occ_retention,
    occ_limit,
    agg_retention,
    agg_limit,
):
    ev_rows, loc_cols = intensity_bin.shape
    curve_count, knot_count = curves.shape
    contract_count = occ_retention.shape[0]
    share = contract_count // lax.axis_size("loc")
    class_onehot = (
        location_class[:, None] == jnp.arange(curve_count, dtype=jnp.int32)[None, :]
    ).astype(jnp.float32)
    knot_table = lax.dot_general(
        curves,
        class_onehot,
        (((0,), (1,)), ((), ())),
        precision=lax.Precision.HIGHEST,
        preferred_element_type=jnp.float32,
    )
    knot_index = jnp.arange(knot_count, dtype=jnp.int32)[None, :, None]
    rows_step = math.gcd(ev_rows, 16)
    step_count = ev_rows // rows_step
    mask_cols = footprint_mask.shape[1]

    def damage_rows(pieces):
        bins, frac, mask = pieces
        weight = frac.astype(jnp.float32)[:, None, :]
        bins_wide = bins[:, None, :]
        hats = jnp.where(bins_wide == knot_index, 1.0 - weight, 0.0) + jnp.where(
            bins_wide + 1 == knot_index, weight, 0.0
        )
        damage = jnp.sum(hats * knot_table[None, :, :], axis=1)
        blocks = (
            damage.reshape(rows_step, mask_cols, loc_cols // mask_cols)
            * mask.astype(jnp.float32)[:, :, None]
        )
        return (blocks.reshape(rows_step, loc_cols) * exposure[None, :]).astype(jnp.bfloat16)

    loss = lax.map(
        damage_rows,
        (
            intensity_bin.reshape(step_count, rows_step, loc_cols),
            bin_fraction.reshape(step_count, rows_step, loc_cols),
            footprint_mask.reshape(step_count, rows_step, mask_cols),
        ),
    ).reshape(ev_rows, loc_cols)
    first = lax.axis_index("loc") * share
    width = math.gcd(lax.axis_size("loc") * share, 256)
    pieces = lax.axis_size("loc") * share // width

    def one_piece(which):
        member = (
            location_contract[:, None]
            == which * width + jnp.arange(width, dtype=jnp.int32)[None, :]
        ).astype(jnp.bfloat16)
        return lax.dot_general(
            member, loss, (((0,), (1,)), ((), ())), preferred_element_type=jnp.float32
        )

    totals = lax.psum_scatter(
        lax.map(one_piece, jnp.arange(pieces, dtype=jnp.int32)).reshape(
            lax.axis_size("loc") * share, ev_rows
        ),
        "loc",
        scatter_dimension=0,
        tiled=True,
    )
    own_ret = lax.dynamic_slice_in_dim(occ_retention, first, share, 0)
    own_lim = lax.dynamic_slice_in_dim(occ_limit, first, share, 0)
    own_aret = lax.dynamic_slice_in_dim(agg_retention, first, share, 0)
    own_alim = lax.dynamic_slice_in_dim(agg_limit, first, share, 0)
    occurrence = jnp.minimum(jnp.maximum(totals - own_ret[:, None], 0.0), own_lim[:, None])
    year_count = YR_DEV * lax.axis_size("ev")
    year_onehot = (event_year[:, None] == jnp.arange(year_count, dtype=jnp.int32)[None, :]).astype(
        jnp.float32
    )
    partial_years = jnp.dot(
        occurrence, year_onehot, precision=lax.Precision.HIGHEST, preferred_element_type=jnp.float32
    )
    yearly = lax.psum_scatter(partial_years, "ev", scatter_dimension=1, tiled=True)
    annual = jnp.minimum(jnp.maximum(yearly - own_aret[:, None], 0.0), own_alim[:, None])
    year_mean = lax.psum(jnp.sum(annual, axis=0), "loc") / contract_count
    return (annual, year_mean)


def solution(mesh):
    in_specs = (
        P("ev", ("grp", "loc")),
        P("ev", ("grp", "loc")),
        P("ev", ("grp", "loc")),
        P(("grp", "loc")),
        P(("grp", "loc")),
        P(("grp", "loc")),
        P(),
        P("ev"),
        P("grp"),
        P("grp"),
        P("grp"),
        P("grp"),
    )
    out_specs = (P(("grp", "loc"), "ev"), P(("grp", "ev")))
    return jax.shard_map(local, mesh=mesh, in_specs=in_specs, out_specs=out_specs, check_vma=False)
```

profile of v0, /device:TPU:0, one launch (start us, length us, event | category | flops | bytes accessed | tf_op | source)
XLA Modules:
  0.0 134.6 jit_solution(8424766924364381948)
XLA Ops:
  8.0 1.2 convolution_bitcast_fusion.1
  9.2 34.5 %while.23 = (s32[]{:T(128)}, bf16[8,16,1024]{2,1,0:T(8,128)(2,1)S(1)}, s32[8,16,1024]{2,1,0:T(8,128)}, bf16[8,16,1024]{2,1,0:T(8,128)(2,1)}, f32[64,1024]{1,0:T(...) while((s32[]{:T(128)}, bf16[8,16,1024]{2,1,0:T(8,128)(2,1)S(1)}, ...), condition=%wide.region_2.3_spmd.clone.clone, body=%wide.region_0.2_spmd.clone.clone.sunk | while | flops 7438466 | bytes 1367693 | solution.py:58
  9.5 0.8 bitcast_convert_fusion.2
  10.2 0.8 broadcast_add_fusion.2
  11.1 0.8 broadcast_subtract_fusion.2
  11.9 1.6 %multiply_reduce_fusion.2 = f32[16,1024]{1,0:T(8,128)S(1)} fusion(f32[64,1024]{1,0:T(8,128)S(1)} %get-tuple-element.252, f32[16,1024]{1,0:T(8,128)S(1)} %bitcast_convert_fusion.2, s32[16,1024]{1,0:T(8,128)S(1)} %get-tuple-element.230, f32[16,1024]{1,0:T(8,128)S(1)} %broadcast_subtract_fusion.2, s32[16,1024]{1,0:T(8,128)S(1)} %get-tuple-element.231), kind=kLoop, calls=%fused_computation.9.clone.1 | loop fusion | flops 7323648 | bytes 589824 | tf_op jit(solution)/shard_map/while/body/eval_jaxpr/reduce_sum | solution.py:51
  13.8 0.8 bitcast_convert_fusion.2
  14.6 0.8 broadcast_add_fusion.2
  15.4 0.8 broadcast_subtract_fusion.2
  16.2 1.6 %multiply_reduce_fusion.2 = f32[16,1024]{1,0:T(8,128)S(1)} fusion(f32[64,1024]{1,0:T(8,128)S(1)} %get-tuple-element.252, f32[16,1024]{1,0:T(8,128)S(1)} %bitcast_convert_fusion.2, s32[16,1024]{1,0:T(8,128)S(1)} %get-tuple-element.230, f32[16,1024]{1,0:T(8,128)S(1)} %broadcast_subtract_fusion.2, s32[16,1024]{1,0:T(8,128)S(1)} %get-tuple-element.231), kind=kLoop, calls=%fused_computation.9.clone.1 | loop fusion | flops 7323648 | bytes 589824 | tf_op jit(solution)/shard_map/while/body/eval_jaxpr/reduce_sum | solution.py:51
  18.1 0.8 bitcast_convert_fusion.2
  18.9 0.8 broadcast_add_fusion.2
  19.7 0.8 broadcast_subtract_fusion.2
  20.5 1.6 %multiply_reduce_fusion.2 = f32[16,1024]{1,0:T(8,128)S(1)} fusion(f32[64,1024]{1,0:T(8,128)S(1)} %get-tuple-element.252, f32[16,1024]{1,0:T(8,128)S(1)} %bitcast_convert_fusion.2, s32[16,1024]{1,0:T(8,128)S(1)} %get-tuple-element.230, f32[16,1024]{1,0:T(8,128)S(1)} %broadcast_subtract_fusion.2, s32[16,1024]{1,0:T(8,128)S(1)} %get-tuple-element.231), kind=kLoop, calls=%fused_computation.9.clone.1 | loop fusion | flops 7323648 | bytes 589824 | tf_op jit(solution)/shard_map/while/body/eval_jaxpr/reduce_sum | solution.py:51
  22.4 0.8 bitcast_convert_fusion.2
  23.2 0.8 broadcast_add_fusion.2
  24.0 0.8 broadcast_subtract_fusion.2
  24.8 1.6 %multiply_reduce_fusion.2 = f32[16,1024]{1,0:T(8,128)S(1)} fusion(f32[64,1024]{1,0:T(8,128)S(1)} %get-tuple-element.252, f32[16,1024]{1,0:T(8,128)S(1)} %bitcast_convert_fusion.2, s32[16,1024]{1,0:T(8,128)S(1)} %get-tuple-element.230, f32[16,1024]{1,0:T(8,128)S(1)} %broadcast_subtract_fusion.2, s32[16,1024]{1,0:T(8,128)S(1)} %get-tuple-element.231), kind=kLoop, calls=%fused_computation.9.clone.1 | loop fusion | flops 7323648 | bytes 589824 | tf_op jit(solution)/shard_map/while/body/eval_jaxpr/reduce_sum | solution.py:51
  26.7 0.8 bitcast_convert_fusion.2
  27.5 0.8 broadcast_add_fusion.2
  28.3 0.8 broadcast_subtract_fusion.2
  29.1 1.6 %multiply_reduce_fusion.2 = f32[16,1024]{1,0:T(8,128)S(1)} fusion(f32[64,1024]{1,0:T(8,128)S(1)} %get-tuple-element.252, f32[16,1024]{1,0:T(8,128)S(1)} %bitcast_convert_fusion.2, s32[16,1024]{1,0:T(8,128)S(1)} %get-tuple-element.230, f32[16,1024]{1,0:T(8,128)S(1)} %broadcast_subtract_fusion.2, s32[16,1024]{1,0:T(8,128)S(1)} %get-tuple-element.231), kind=kLoop, calls=%fused_computation.9.clone.1 | loop fusion | flops 7323648 | bytes 589824 | tf_op jit(solution)/shard_map/while/body/eval_jaxpr/reduce_sum | solution.py:51
  31.0 0.8 bitcast_convert_fusion.2
  31.8 0.8 broadcast_add_fusion.2
  32.6 0.8 broadcast_subtract_fusion.2
  33.4 1.6 %multiply_reduce_fusion.2 = f32[16,1024]{1,0:T(8,128)S(1)} fusion(f32[64,1024]{1,0:T(8,128)S(1)} %get-tuple-element.252, f32[16,1024]{1,0:T(8,128)S(1)} %bitcast_convert_fusion.2, s32[16,1024]{1,0:T(8,128)S(1)} %get-tuple-element.230, f32[16,1024]{1,0:T(8,128)S(1)} %broadcast_subtract_fusion.2, s32[16,1024]{1,0:T(8,128)S(1)} %get-tuple-element.231), kind=kLoop, calls=%fused_computation.9.clone.1 | loop fusion | flops 7323648 | bytes 589824 | tf_op jit(solution)/shard_map/while/body/eval_jaxpr/reduce_sum | solution.py:51
  35.3 0.8 bitcast_convert_fusion.2
  36.1 0.8 broadcast_add_fusion.2
  36.9 0.8 broadcast_subtract_fusion.2
  37.7 1.6 %multiply_reduce_fusion.2 = f32[16,1024]{1,0:T(8,128)S(1)} fusion(f32[64,1024]{1,0:T(8,128)S(1)} %get-tuple-element.252, f32[16,1024]{1,0:T(8,128)S(1)} %bitcast_convert_fusion.2, s32[16,1024]{1,0:T(8,128)S(1)} %get-tuple-element.230, f32[16,1024]{1,0:T(8,128)S(1)} %broadcast_subtract_fusion.2, s32[16,1024]{1,0:T(8,128)S(1)} %get-tuple-element.231), kind=kLoop, calls=%fused_computation.9.clone.1 | loop fusion | flops 7323648 | bytes 589824 | tf_op jit(solution)/shard_map/while/body/eval_jaxpr/reduce_sum | solution.py:51
  39.6 0.8 bitcast_convert_fusion.2
  40.4 0.8 broadcast_add_fusion.2
  41.3 0.8 broadcast_subtract_fusion.2
  42.0 1.6 %multiply_reduce_fusion.2 = f32[16,1024]{1,0:T(8,128)S(1)} fusion(f32[64,1024]{1,0:T(8,128)S(1)} %get-tuple-element.252, f32[16,1024]{1,0:T(8,128)S(1)} %bitcast_convert_fusion.2, s32[16,1024]{1,0:T(8,128)S(1)} %get-tuple-element.230, f32[16,1024]{1,0:T(8,128)S(1)} %broadcast_subtract_fusion.2, s32[16,1024]{1,0:T(8,128)S(1)} %get-tuple-element.231), kind=kLoop, calls=%fused_computation.9.clone.1 | loop fusion | flops 7323648 | bytes 589824 | tf_op jit(solution)/shard_map/while/body/eval_jaxpr/reduce_sum | solution.py:51
  43.7 19.5 %while.22 = (s32[]{:T(128)}, f32[8,256,128]{2,1,0:T(8,128)}, s32[1024]{0:T(1024)S(1)}, s32[8]{0:T(128)S(1)}, bf16[128,1024]{1,0:T(8,128)(2,1)S(1)}, /*index=5*/s32[]{:T(128)}, s32[1]{0:T(128)}) while((s32[]{:T(128)}, f32[8,256,128]{2,1,0:T(8,128)}, s32[1024]{0:T(1024)S(1)}, s32[8]{0:T(128)S(1)}, bf16[128,1024]{1,0:T(8,128)(2,1)S(1)}, ...), condition=%wide.region_4.5_spmd, body=%wide.region_3.4_spmd.sunk | while | flops 67633408 | bytes 399477 | solution.py:80
  45.0 1.2 fusion.25
  47.4 1.2 fusion.25
  49.8 1.2 fusion.25
  52.3 1.2 fusion.25
  54.7 1.2 fusion.25
  57.2 1.2 fusion.25
  59.6 1.2 fusion.25
  62.0 1.2 fusion.25
  64.8 33.9 %reduce-scatter.3.cloned.1.call-done = f32[256,128]{1,0:T(8,128)} async-done(((f32[2048,128]{1,0:T(8,128)}), f32[256,128]{1,0:T(8,128)}) %reduce-scatter.3.cloned.1.call-update) | async-done | bytes 131088 | tf_op jit(solution)/shard_map/reduce_scatter | solution.py:79
  98.7 1.9 %fusion.9 = f32[256,128]{0,1:T(8,128)} fusion(f32[256,128]{1,0:T(8,128)} %reduce-scatter.3.cloned.1.call-done, f32[256]{0:T(256)S(1)} %dynamic_slice.29, f32[256]{0:T(256)S(1)} %dynamic_slice.28, s32[128]{0:T(128)S(1)} %copy-done.2), kind=kOutput, calls=%fused_computation.23 | convolution fusion | flops 50446336 | bytes 264704 | tf_op jit(solution)/shard_map/dot_general | solution.py:96
  102.2 7.4 %reduce-scatter.5.cloned.1.call-done = f32[256,64]{0,1:T(8,128)} async-done(((f32[256,128]{0,1:T(8,128)}), f32[256,64]{0,1:T(8,128)}) %reduce-scatter.5.cloned.1.call-update) | async-done | bytes 65552 | tf_op jit(solution)/shard_map/reduce_scatter | solution.py:99
  109.5 1.6 %fusion.18 = (f32[64]{0:T(128)S(1)}, f32[256,64]{0,1:T(8,128)}) fusion(f32[256]{0:T(256)S(1)} %dynamic_slice.31, f32[256,64]{0,1:T(8,128)} %reduce-scatter.5.cloned.1.call-done, f32[256]{0:T(256)S(1)} %dynamic_slice.30), kind=kLoop, calls=%fused_computation.35 | loop fusion | flops 65472 | bytes 133376 | tf_op jit(solution)/shard_map/reduce_sum | solution.py:101
  111.1 16.1 %psum.7 = f32[64]{0:T(128)S(1)} all-reduce(f32[64]{0:T(128)S(1)} %get-tuple-element.152), channel_id=1, replica_groups=mesh['grp'=2,'ev'=2,'loc'=8] {'loc'}, use_global_device_ids=true, to_apply=%region_8.9 | all-reduce | flops 64 | bytes 512 | tf_op jit(solution)/shard_map/psum | solution.py:101
  (99 shorter events, 10.8 us)
Async XLA Ops:
  7.2 0.8 copy-start
  7.2 91.5 %reduce-scatter.3.cloned.1.call-start = ((), (), s32[]{:S(2)}) async-start(), calls=%async_computation.2 | async-start | bytes 1179648 | tf_op jit(solution)/shard_map/reduce_scatter | solution.py:79
  9.2 34.5 %copy-start.3 = (s32[1024]{0:T(1024)S(1)}, s32[1024]{0:T(1024)}, u32[]{:S(2)}) copy-start(s32[1024]{0:T(1024)} %param.19) | copy-start | bytes 12292
  9.3 4.3 %copy-start.1 = (f32[1024]{0:T(1024)S(1)}, f32[1024]{0:T(1024)}, u32[]{:S(2)}) copy-start(f32[1024]{0:T(1024)} %get-tuple-element.254) | copy-start | bytes 12292 | tf_op jit(solution)/shard_map/while
  13.6 4.3 %copy-start.1 = (f32[1024]{0:T(1024)S(1)}, f32[1024]{0:T(1024)}, u32[]{:S(2)}) copy-start(f32[1024]{0:T(1024)} %get-tuple-element.254) | copy-start | bytes 12292 | tf_op jit(solution)/shard_map/while
  17.9 4.3 %copy-start.1 = (f32[1024]{0:T(1024)S(1)}, f32[1024]{0:T(1024)}, u32[]{:S(2)}) copy-start(f32[1024]{0:T(1024)} %get-tuple-element.254) | copy-start | bytes 12292 | tf_op jit(solution)/shard_map/while
  22.2 4.3 %copy-start.1 = (f32[1024]{0:T(1024)S(1)}, f32[1024]{0:T(1024)}, u32[]{:S(2)}) copy-start(f32[1024]{0:T(1024)} %get-tuple-element.254) | copy-start | bytes 12292 | tf_op jit(solution)/shard_map/while
  26.5 4.3 %copy-start.1 = (f32[1024]{0:T(1024)S(1)}, f32[1024]{0:T(1024)}, u32[]{:S(2)}) copy-start(f32[1024]{0:T(1024)} %get-tuple-element.254) | copy-start | bytes 12292 | tf_op jit(solution)/shard_map/while
  30.8 4.3 %copy-start.1 = (f32[1024]{0:T(1024)S(1)}, f32[1024]{0:T(1024)}, u32[]{:S(2)}) copy-start(f32[1024]{0:T(1024)} %get-tuple-element.254) | copy-start | bytes 12292 | tf_op jit(solution)/shard_map/while
  35.1 4.3 %copy-start.1 = (f32[1024]{0:T(1024)S(1)}, f32[1024]{0:T(1024)}, u32[]{:S(2)}) copy-start(f32[1024]{0:T(1024)} %get-tuple-element.254) | copy-start | bytes 12292 | tf_op jit(solution)/shard_map/while
  39.4 4.3 %copy-start.1 = (f32[1024]{0:T(1024)S(1)}, f32[1024]{0:T(1024)}, u32[]{:S(2)}) copy-start(f32[1024]{0:T(1024)} %get-tuple-element.254) | copy-start | bytes 12292 | tf_op jit(solution)/shard_map/while
  63.2 35.5 %copy-start.2 = (s32[128]{0:T(128)S(1)}, s32[128]{0:T(128)}, u32[]{:S(2)}) copy-start(s32[128]{0:T(128)} %param.23) | copy-start | bytes 1540
  63.2 46.3 %reduce-scatter.5.cloned.1.call-start = ((), (), s32[]{:S(2)}) async-start(), calls=%async_computation.3 | async-start | bytes 196608 | tf_op jit(solution)/shard_map/reduce_scatter | solution.py:99
Sparse Core Ops, SparseCore 0:
  63.4 35.2 reduce-scatter.2
  100.9 8.5 reduce-scatter.4
where the time goes:
time: 137 us; the launch traced here: 135 us
  waiting for transfers between devices  41.3 us (30%)
  other arithmetic  34.6 us (25%)
  blocking collectives  16.1 us (12%)
  between operations  14.1 us (10%)
  matrix products  12.6 us (9%)
  local copies, waits for them, and re-layouts  9.98 us (7%)
  loops' own time  5.83 us (4%)
    reduce_scatter x1, waiting for transfers between devices, local(): lax.psum_scatter(lax.map(one_piece, jnp.arange(pieces, dtype=jnp.int32))....  33.9 us
    psum x1, blocking collectives, local(): year_mean = lax.psum(jnp.sum(annual, axis=0), 'loc') / contract_count  16.1 us
    reduce_sum x8, other arithmetic, damage_rows(): damage = jnp.sum(hats * knot_table[None, :, :], axis=1)  13.1 us
    dot_general x8, matrix products, one_piece(): lax.dot_general(member, loss, (((0,), (1,)), ((), ())), preferred_element...  9.5 us
    reduce_scatter x1, waiting for transfers between devices, local(): lax.psum_scatter(partial_years, 'ev', scatter_dimension=1, tiled=True)  7.39 us
    add x8, other arithmetic, damage_rows(): bins_wide + 1 == knot_index  6.79 us
    sub x8, other arithmetic, damage_rows(): 1.0 - weight  6.17 us
    convert_element_type x8, other arithmetic, damage_rows(): weight = frac.astype(jnp.float32)[:, None, :]  6.16 us
  transfers between devices with their start and end apart: 2, of which 2 were waited for; matrix products, arithmetic and copies ran while one was open for 2% of the time, Pallas kernels for 0%

commit v1 on v0

v1 whole, which is shorter than its diff:
```python
import functools

import jax
import jax.numpy as jnp
from jax import lax
from jax.experimental import pallas as pl
from jax.experimental.pallas import tpu as pltpu
from jax.sharding import PartitionSpec as P

YR_DEV = 64
LANES = 128
SUBLANES = 8
CORES = 2

f32, bf16, i32 = jnp.float32, jnp.bfloat16, jnp.int32
HBM = pl.BlockSpec(memory_space=pltpu.HBM)
VMEM = pl.BlockSpec(memory_space=pltpu.VMEM)


def split3(x):
    a = x.astype(bf16)
    rest = x - a.astype(f32)
    b = rest.astype(bf16)
    rest = rest - b.astype(f32)
    return a, b, rest.astype(bf16)


def take_rows(x, index):
    return jnp.take_along_axis(x, index, axis=0, mode="promise_in_bounds")


def start_all(pairs, sems):
    copies = [pltpu.make_async_copy(src, dst, sems.at[i]) for i, (src, dst) in enumerate(pairs)]
    for copy in copies:
        copy.start()
    return copies


def member_rows(contract_ref, first, share):
    rows = lax.broadcasted_iota(i32, (share, LANES), 0)
    return jnp.concatenate(
        [
            (rows == contract_ref[j : j + 1, :] - first).astype(bf16)
            for j in range(contract_ref.shape[0])
        ],
        axis=1,
    )


def block_totals(contract_ref, loss, first, share):
    return lax.dot_general(
        loss,
        member_rows(contract_ref, first, share),
        (((1,), (1,)), ((), ())),
        preferred_element_type=f32,
    )


def damage_kernel(
    share, parts, bins_h, frac_h, mask_h, class_h, exposure_h, curve_h, contract_h,
    year_h, send_ref, loss_ref, contract_s, year_s,
    bins, frac, mask_s, class_s, exposure_s, curve_s, table, sems,
):
    events, locations = bins.shape
    knots, curves = curve_s.shape
    tiles = locations // LANES
    width = locations // parts
    small = start_all(
        [(class_h, class_s), (curve_h, curve_s), (mask_h, mask_s), (exposure_h, exposure_s),
         (contract_h, contract_s), (year_h, year_s)],
        sems,
    )
    large = start_all(
        [
            (src.at[:, p * width : (p + 1) * width], dst.at[:, p * width : (p + 1) * width])
            for p in range(parts)
            for src, dst in ((bins_h, bins), (frac_h, frac))
        ],
        sems.at[pl.ds(len(small), 2 * parts)],
    )
    for copy in small:
        copy.wait()
    low = curve_s[...]
    high = jnp.concatenate([low[1:], low[:1]], axis=0)
    terms = jnp.concatenate(split3(jnp.concatenate([low, high], axis=0)), axis=1)
    for j in range(tiles):
        onehot = (
            lax.broadcasted_iota(i32, (curves, LANES), 0) == class_s[j : j + 1, :]
        ).astype(bf16)
        table[:, j * LANES : (j + 1) * LANES] = jnp.dot(
            terms, jnp.concatenate([onehot] * 3, axis=0), preferred_element_type=f32
        )
    mask = mask_s[...].astype(f32).T
    groups = knots // SUBLANES
    for j in range(tiles):
        if j % (tiles // parts) == 0:
            for copy in large[2 * (j // (tiles // parts)) :][:2]:
                copy.wait()
        cols = slice(j * LANES, (j + 1) * LANES)
        lows = [table[SUBLANES * v : SUBLANES * (v + 1), cols] for v in range(groups)]
        highs = [
            table[knots + SUBLANES * v : knots + SUBLANES * (v + 1), cols] for v in range(groups)
        ]
        exposure = jnp.broadcast_to(exposure_s[j : j + 1, :], (SUBLANES, LANES))
        out = []
        for i in range(events // SUBLANES):
            rows = slice(SUBLANES * i, SUBLANES * (i + 1))
            knot = bins[rows, cols]
            within = knot & (SUBLANES - 1)
            group = knot // SUBLANES
            bits = [(group & (1 << q)) != 0 for q in range((groups - 1).bit_length())]

            def pick(tables):
                values = [take_rows(x, within) for x in tables]
                for bit in bits:
                    pairs = [values[q : q + 2] for q in range(0, len(values), 2)]
                    values = [jnp.where(bit, p[1], p[0]) if len(p) == 2 else p[0] for p in pairs]
                return values[0]

            weight = frac[rows, cols].astype(f32)
            damage = (1.0 - weight) * pick(lows) + weight * pick(highs)
            keep = jnp.broadcast_to(mask[rows, j : j + 1], (SUBLANES, LANES))
            out.append(damage * keep * exposure)
        loss_ref[:, cols] = jnp.concatenate(out, axis=0).astype(bf16)
    loc_count = lax.axis_size("loc")
    chips = loc_count // CORES
    me = lax.axis_index("loc")
    chip, core = me // CORES, lax.rem(me, CORES)
    loss = loss_ref[...]
    for k in range(chips):
        owner = lax.rem(chip + k, chips) * CORES + (1 - core)
        send_ref[k] = block_totals(contract_s, loss, owner * share, share)


def own_kernel(share, contract_s, loss_ref, out_ref):
    chips = out_ref.shape[0]
    me = lax.axis_index("loc")
    chip, core = me // CORES, lax.rem(me, CORES)
    loss = loss_ref[...]
    for k in range(chips):
        owner = lax.rem(chip + k, chips) * CORES + core
        out_ref[k] = block_totals(contract_s, loss, owner * share, share)


def year_kernel(count, *refs):
    ins, (terms_ref, year_ref), outs = (
        refs[:count], refs[count : count + 2], refs[count + 2 :]
    )
    total = ins[0][...]
    for ref in ins[1:]:
        total = total + ref[...]
    occurrence = jnp.minimum(jnp.maximum(total - terms_ref[0:1, :], 0.0), terms_ref[1:2, :])
    evs = len(outs)
    events = total.shape[0]
    ev = lax.axis_index("ev")
    for m, out in enumerate(outs):
        first = lax.rem(ev + m, evs) * YR_DEV
        years = lax.broadcasted_iota(i32, (YR_DEV, events), 0) + first
        onehot = (years == year_ref[...]).astype(f32)
        out[...] = jnp.dot(
            onehot, occurrence, precision=lax.Precision.HIGHEST, preferred_element_type=f32
        )


def annual_kernel(count, *refs):
    ins, (terms_ref, annual_ref, part_ref) = refs[:count], refs[count:]
    yearly = ins[0][...]
    for ref in ins[1:]:
        yearly = yearly + ref[...]
    annual = jnp.minimum(jnp.maximum(yearly - terms_ref[2:3, :], 0.0), terms_ref[3:4, :])
    annual_ref[...] = annual
    ones = jnp.ones((SUBLANES, annual.shape[1]), f32)
    part = lax.dot_general(
        ones, annual, (((1,), (1,)), ((), ())),
        precision=lax.Precision.HIGHEST, preferred_element_type=f32,
    )
    part_ref[...] = part[0:1, :]


def params(mib):
    return pltpu.CompilerParams(vmem_limit_bytes=mib << 20)


def rotate(size, k):
    return [(i, (i + k) % size) for i in range(size)]


def local(
    intensity_bin, bin_fraction, footprint_mask, location_contract, location_class, exposure,
    curves, event_year, occ_retention, occ_limit, agg_retention, agg_limit,
):
    events, locations = intensity_bin.shape
    curve_count, knots = curves.shape
    contract_count = occ_retention.shape[0]
    loc_count = lax.axis_size("loc")
    evs = lax.axis_size("ev")
    chips = loc_count // CORES
    share = contract_count // loc_count
    tiles = locations // LANES
    parts = 4
    dma = pltpu.SemaphoreType.DMA
    send, loss, contract_v, year_v = pl.pallas_call(
        functools.partial(damage_kernel, share, parts),
        out_shape=(
            jax.ShapeDtypeStruct((chips, events, share), f32),
            jax.ShapeDtypeStruct((events, locations), bf16),
            jax.ShapeDtypeStruct((tiles, LANES), i32),
            jax.ShapeDtypeStruct((1, events), i32),
        ),
        in_specs=[HBM] * 8,
        out_specs=(VMEM,) * 4,
        scratch_shapes=[
            pltpu.VMEM((events, locations), i32),
            pltpu.VMEM((events, locations), bf16),
            pltpu.VMEM((tiles, events), i32),
            pltpu.VMEM((tiles, LANES), i32),
            pltpu.VMEM((tiles, LANES), f32),
            pltpu.VMEM((knots, curve_count), f32),
            pltpu.VMEM((2 * knots, locations), f32),
            dma((6 + 2 * parts,)),
        ],
        compiler_params=params(24),
        cost_estimate=pl.CostEstimate(flops=10**9, bytes_accessed=2 << 20, transcendentals=0),
        name="damage",
    )(
        *(
            pltpu.with_memory_space_constraint(x, pltpu.HBM)
            for x in (
                intensity_bin, bin_fraction, footprint_mask.T,
                location_class.reshape(tiles, LANES), exposure.reshape(tiles, LANES), curves.T,
                location_contract.reshape(tiles, LANES), event_year.reshape(1, events),
            )
        )
    )
    partner = [(i, i ^ 1) for i in range(loc_count)]
    got = lax.ppermute(send, "loc", partner)
    own = pl.pallas_call(
        functools.partial(own_kernel, share),
        out_shape=jax.ShapeDtypeStruct((chips, events, share), f32),
        in_specs=[VMEM, VMEM],
        out_specs=VMEM,
        compiler_params=params(16),
        cost_estimate=pl.CostEstimate(flops=10**9, bytes_accessed=2 << 20, transcendentals=0),
        name="own_part",
    )(contract_v, loss)
    blocks = [own[0], got[0]]
    for k in range(chips - 1, 0, -1):
        pairs = [
            (i, ((i // CORES + k) % chips) * CORES + i % CORES) for i in range(loc_count)
        ]
        blocks.append(lax.ppermute(own[k] + got[k], "loc", pairs))
    first = lax.axis_index("loc") * share
    terms = lax.dynamic_slice(
        jnp.stack([occ_retention, occ_limit, agg_retention, agg_limit]), (0, first), (4, share)
    )
    yearly = pl.pallas_call(
        functools.partial(year_kernel, len(blocks)),
        out_shape=tuple(jax.ShapeDtypeStruct((YR_DEV, share), f32) for _ in range(evs)),
        in_specs=[VMEM] * (len(blocks) + 2),
        out_specs=tuple(VMEM for _ in range(evs)),
        compiler_params=params(16),
        name="years",
    )(*blocks, terms, year_v)
    sums = [yearly[0]] + [
        lax.ppermute(yearly[m], "ev", rotate(evs, m)) for m in range(1, evs)
    ]
    annual, part = pl.pallas_call(
        functools.partial(annual_kernel, len(sums)),
        out_shape=(
            jax.ShapeDtypeStruct((YR_DEV, share), f32),
            jax.ShapeDtypeStruct((1, YR_DEV), f32),
        ),
        in_specs=[VMEM] * (len(sums) + 1),
        out_specs=(VMEM, VMEM),
        compiler_params=params(16),
        name="annual",
    )(*sums, terms)
    mean = part.reshape(YR_DEV)
    if loc_count & (loc_count - 1) == 0:
        step = 1
        while step < loc_count:
            mean = mean + lax.ppermute(mean, "loc", [(i, i ^ step) for i in range(loc_count)])
            step *= 2
    else:
        mean = lax.psum(mean, "loc")
    return annual.T, mean / contract_count


def solution(mesh):
    in_specs = (
        P("ev", ("grp", "loc")),
        P("ev", ("grp", "loc")),
        P("ev", ("grp", "loc")),
        P(("grp", "loc")),
        P(("grp", "loc")),
        P(("grp", "loc")),
        P(),
        P("ev"),
        P("grp"),
        P("grp"),
        P("grp"),
        P("grp"),
    )
    out_specs = (P(("grp", "loc"), "ev"), P(("grp", "ev")))
    return jax.shard_map(local, mesh=mesh, in_specs=in_specs, out_specs=out_specs, check_vma=False)
```

time: 137 us -> 37.9 us (0.28); the launches traced: 135 us -> 37.7 us
  other arithmetic: 34.6 us -> 0.67 us
  waiting for transfers between devices: 41.3 us -> 19.5 us
  blocking collectives: 16.1 us -> 0 us
  between operations: 14.1 us -> 0.68 us
  matrix products: 12.6 us -> 0 us
  starting transfers between devices: 0.08 us -> 11.2 us
  local copies, waits for them, and re-layouts: 9.98 us -> 0.71 us
  loops' own time: 5.83 us -> 0 us
  Pallas kernels: 0 us -> 5 us
    reduce_scatter x2 -> x0, waiting for transfers between devices: 41.3 us -> none  [the longest x1 33.9 us: local(): lax.psum_scatter(lax.map(one_piece, jnp.arange(pieces, dtype=jnp.int32))....]
    ppermute x0 -> x8, waiting for transfers between devices: none -> 19.5 us  [the longest x3 9.86 us: local(): blocks.append(lax.ppermute(own[k] + got[k], 'loc', pairs))]
    psum x1 -> x0, blocking collectives: 16.1 us -> none  [local(): year_mean = lax.psum(jnp.sum(annual, axis=0), 'loc') / contract_count]
    reduce_sum x9 -> x0, other arithmetic: 14.7 us -> none  [the longest x8 13.1 us: damage_rows(): damage = jnp.sum(hats * knot_table[None, :, :], axis=1)]
    dot_general x10 -> x0, matrix products: 12.6 us -> none  [the longest x8 9.5 us: one_piece(): lax.dot_general(member, loss, (((0,), (1,)), ((), ())), preferred_element...]
    ppermute x0 -> x8, starting transfers between devices: none -> 11.2 us  [the longest x3 6.02 us: local(): blocks.append(lax.ppermute(own[k] + got[k], 'loc', pairs))]
    dynamic_slice x20 -> x0, local copies, waits for them, and re-layouts: 7.78 us -> none  [the longest x8 4.66 us: local(): lax.map(one_piece, jnp.arange(pieces, dtype=jnp.int32))]
    add x16 -> x3, other arithmetic: 6.82 us -> 0.07 us  [the longest x1 0.07 us: local(): blocks.append(lax.ppermute(own[k] + got[k], 'loc', pairs))]
  transfers between devices with their start and end apart: 2 -> 8, of which waited for: 2 -> 7; matrix products, arithmetic and copies ran while one was open for 2% -> 0% of each run, Pallas kernels for 0% -> 2%
where the time goes in v1:
time: 37.9 us; the launch traced here: 37.7 us
  waiting for transfers between devices  19.5 us (51%)
  starting transfers between devices  11.2 us (30%)
  Pallas kernels  5 us (13%)
  local copies, waits for them, and re-layouts  0.71 us (2%)
  between operations  0.68 us (2%)
  other arithmetic  0.67 us (2%)
    ppermute x3, waiting for transfers between devices, local(): blocks.append(lax.ppermute(own[k] + got[k], 'loc', pairs))  9.86 us
    ppermute x3, waiting for transfers between devices, local(): lax.ppermute(mean, 'loc', [(i, i ^ step) for i in range(loc_count)])  6.13 us
    ppermute x3, starting transfers between devices, local(): blocks.append(lax.ppermute(own[k] + got[k], 'loc', pairs))  6.02 us
    pallas_call x1, Pallas kernels, local(): pl.pallas_call(functools.partial(damage_kernel, share, parts), out_shape=...  3.24 us
    ppermute x3, starting transfers between devices, local(): lax.ppermute(mean, 'loc', [(i, i ^ step) for i in range(loc_count)])  3.07 us
    ppermute x1, waiting for transfers between devices, local(): lax.ppermute(yearly[m], 'ev', rotate(evs, m))  2.78 us
    ppermute x1, starting transfers between devices, local(): lax.ppermute(yearly[m], 'ev', rotate(evs, m))  1.55 us
    pallas_call x1, Pallas kernels, local(): pl.pallas_call(functools.partial(own_kernel, share), out_shape=jax.ShapeD...  0.83 us
  transfers between devices with their start and end apart: 8, of which 7 were waited for; matrix products, arithmetic and copies ran while one was open for 0% of the time, Pallas kernels for 2%

profile of v1, /device:TPU:0, one launch (start us, length us, event | category | flops | bytes accessed | tf_op | source)
XLA Modules:
  0.0 37.7 jit_solution(2010461828555371137)
XLA Ops:
  0.6 3.2 %damage.1 = (f32[4,128,256]{2,1,0:T(8,128)S(1)}, bf16[128,1024]{1,0:T(8,128)(2,1)S(1)}, s32[8,128]{1,0:T(8,128)S(1)}, s32[1,128]{1,0:T(1,128)S(1)}) custom-call(s32[128,1024]{1,0:T(8,128)} %bins_h.1, bf16[128,1024]{1,0:T(8,128)(2,1)} %frac_h.1, s32[8,128]{1,0:T(8,128)} %bitcast.30, s32[8,128]{1,0:T(8,128)} %bitcast.31, f32[8,128]{1,0:T(8,128)} %bitcast.32, ...), custom_call_target="tpu_custom_call" | custom-call | flops 1000000000 | bytes 2097152 | tf_op jit(solution)/shard_map/damage/pallas_call | solution.py:202
  3.9 0.6 %collective-permute-start = (f32[4,128,256]{2,1,0:T(8,128)S(1)}, f32[4,128,256]{2,1,0:T(8,128)S(1)}, u32[]{:S(2)}, u32[]{:S(2)}) collective-permute-start(f32[4,128,256]{2,1,0:T(8,128)S(1)} %get-tuple-element.12), channel_id=1, source_target_pairs={{0,1},{1,0},{2,3},{3,2},{4,5},{5,4},{6,7},{7,6},{8,9},{9,8},{10,11... | collective-permute-start | bytes 1572872 | tf_op jit(solution)/shard_map/ppermute | solution.py:236
  4.4 0.8 %own_part.1 = f32[4,128,256]{2,1,0:T(8,128)S(1)} custom-call(s32[8,128]{1,0:T(8,128)S(1)} %get-tuple-element.10.contract_s, bf16[128,1024]{1,0:T(8,128)(2,1)S(1)} %get-tuple-element.11.loss_ref), custom_call_target="tpu_custom_call" | custom-call | flops 1000000000 | bytes 2097152 | tf_op jit(solution)/shard_map/own_part/pallas_call | solution.py:237
  5.3 0.7 %collective-permute-done = f32[4,128,256]{2,1,0:T(8,128)S(1)} collective-permute-done((f32[4,128,256]{2,1,0:T(8,128)S(1)}, f32[4,128,256]{2,1,0:T(8,128)S(1)}, u32[]{:S(2)}, u32[]{:S(2)}) %collective-permute-start) | collective-permute-done | bytes 524320 | tf_op jit(solution)/shard_map/ppermute | solution.py:236
  6.0 0.0 copy-start.2
  6.0 0.0 copy-start.3
  6.0 0.1 fusion
  6.1 5.0 %collective-permute-start.1 = (f32[128,256]{1,0:T(8,128)S(1)}, f32[128,256]{1,0:T(8,128)S(1)}, u32[]{:S(2)}, u32[]{:S(2)}) collective-permute-start(f32[128,256]{1,0:T(8,128)S(1)} %get-tuple-element.20), channel_id=1, source_target_pairs={{0,6},{1,7},{2,0},{3,1},{4,2},{5,3},{6,4},{7,5},{8,14},{9,15},{10,... | collective-permute-start | bytes 393224 | tf_op jit(solution)/shard_map/ppermute | solution.py:251
  11.1 0.0 collective-permute-start.2
  11.1 1.0 %collective-permute-start.3 = (f32[128,256]{1,0:T(8,128)S(1)}, f32[128,256]{1,0:T(8,128)S(1)}, u32[]{:S(2)}, u32[]{:S(2)}) collective-permute-start(f32[128,256]{1,0:T(8,128)S(1)} %get-tuple-element.18), channel_id=1, source_target_pairs={{0,2},{1,3},{2,4},{3,5},{4,6},{5,7},{6,0},{7,1},{8,10},{9,11},{10,... | collective-permute-start | bytes 393224 | tf_op jit(solution)/shard_map/ppermute | solution.py:251
  12.1 0.0 copy-start.1
  12.1 0.0 copy-start
  12.1 0.0 copy-done.2
  12.1 0.0 copy-done.3
  12.1 0.7 %copy-done.1 = f32[2048]{0:T(1024)S(1)} copy-done((f32[2048]{0:T(1024)S(1)}, f32[2048]{0:T(1024)}, u32[]{:S(2)}) %copy-start.1) | copy-done | bytes 8216
  12.8 0.0 copy-done
  12.8 0.1 fusion.5.refs_5_.refs_2_
  12.9 2.2 %collective-permute-done.1.refs_2_ = f32[128,256]{1,0:T(8,128)S(1)} collective-permute-done((f32[128,256]{1,0:T(8,128)S(1)}, f32[128,256]{1,0:T(8,128)S(1)}, u32[]{:S(2)}, u32[]{:S(2)}) %collective-permute-start.1) | collective-permute-done | bytes 131104 | tf_op jit(solution)/shard_map/ppermute | solution.py:251
  15.0 7.7 %collective-permute-done.2.refs_3_ = f32[128,256]{1,0:T(8,128)S(1)} collective-permute-done((f32[128,256]{1,0:T(8,128)S(1)}, f32[128,256]{1,0:T(8,128)S(1)}, u32[]{:S(2)}, u32[]{:S(2)}) %collective-permute-start.2) | collective-permute-done | bytes 131104 | tf_op jit(solution)/shard_map/ppermute | solution.py:251
  22.7 0.0 collective-permute-done.3.refs_4_
  22.7 0.3 years.1
  23.0 1.6 %collective-permute-start.4 = (f32[64,256]{1,0:T(8,128)S(1)}, f32[64,256]{1,0:T(8,128)S(1)}, u32[]{:S(2)}, u32[]{:S(2)}) collective-permute-start(f32[64,256]{1,0:T(8,128)S(1)} %get-tuple-element.15), channel_id=1, source_target_pairs={{0,8},{8,0},{1,9},{9,1},{2,10},{10,2},{3,11},{11,3},{4,12},{12,4},... | collective-permute-start | bytes 196616 | tf_op jit(solution)/shard_map/ppermute | solution.py:265
  24.6 2.8 %collective-permute-done.4.refs_1_ = f32[64,256]{1,0:T(8,128)S(1)} collective-permute-done((f32[64,256]{1,0:T(8,128)S(1)}, f32[64,256]{1,0:T(8,128)S(1)}, u32[]{:S(2)}, u32[]{:S(2)}) %collective-permute-start.4) | collective-permute-done | bytes 65568 | tf_op jit(solution)/shard_map/ppermute | solution.py:265
  27.4 0.6 %annual.1 = (f32[64,256]{1,0:T(8,128)}, f32[1,64]{1,0:T(1,128)S(1)}) custom-call(f32[64,256]{1,0:T(8,128)S(1)} %get-tuple-element.14.refs_0_, f32[64,256]{1,0:T(8,128)S(1)} %collective-permute-done.4.refs_1_, f32[4,256]{1,0:T(4,128)S(1)} %fusion.5.refs_5_.refs_2_), custom_call_target="tpu_custom_call" | custom-call | tf_op jit(solution)/shard_map/annual/pallas_call | solution.py:267
  28.0 0.0 collective-permute-start.5
  28.0 1.2 %collective-permute-done.5 = f32[64]{0:T(128)S(1)} collective-permute-done((f32[64]{0:T(128)S(1)}, f32[64]{0:T(128)S(1)}, u32[]{:S(2)}, u32[]{:S(2)}) %collective-permute-start.5) | collective-permute-done | bytes 288 | tf_op jit(solution)/shard_map/ppermute | solution.py:282
  29.2 0.6 %collective-permute-start.6 = (f32[64]{0:T(128)S(1)}, f32[64]{0:T(128)S(1)}, u32[]{:S(2)}, u32[]{:S(2)}) collective-permute-start(f32[64]{0:T(128)S(1)} %bitcast_add_fusion), channel_id=1, source_target_pairs={{0,2},{1,3},{2,0},{3,1},{4,6},{5,7},{6,4},{7,5},{8,10},{9,11},{10,... | collective-permute-start | bytes 776 | tf_op jit(solution)/shard_map/ppermute | solution.py:282
  29.8 3.0 %collective-permute-done.6 = f32[64]{0:T(128)S(1)} collective-permute-done((f32[64]{0:T(128)S(1)}, f32[64]{0:T(128)S(1)}, u32[]{:S(2)}, u32[]{:S(2)}) %collective-permute-start.6) | collective-permute-done | bytes 288 | tf_op jit(solution)/shard_map/ppermute | solution.py:282
  32.8 2.5 %collective-permute-start.7 = (f32[64]{0:T(128)S(1)}, f32[64]{0:T(128)S(1)}, u32[]{:S(2)}, u32[]{:S(2)}) collective-permute-start(f32[64]{0:T(128)S(1)} %add.38), channel_id=1, source_target_pairs={{0,4},{1,5},{2,6},{3,7},{4,0},{5,1},{6,2},{7,3},{8,12},{9,13},{10,... | collective-permute-start | bytes 776 | tf_op jit(solution)/shard_map/ppermute | solution.py:282
  35.2 2.0 %collective-permute-done.7 = f32[64]{0:T(128)S(1)} collective-permute-done((f32[64]{0:T(128)S(1)}, f32[64]{0:T(128)S(1)}, u32[]{:S(2)}, u32[]{:S(2)}) %collective-permute-start.7) | collective-permute-done | bytes 288 | tf_op jit(solution)/shard_map/ppermute | solution.py:282
  37.2 0.5 %add_multiply_fusion = f32[64]{0:T(128)} fusion(f32[64]{0:T(128)S(1)} %add.38, f32[64]{0:T(128)S(1)} %collective-permute-done.7), kind=kLoop, calls=%fused_computation.15 | loop fusion | flops 128 | bytes 768 | tf_op jit(solution)/shard_map/div | solution.py:286
  (2 shorter events, 0.0 us)
Async XLA Ops:
  3.9 2.1 %collective-permute-start = (f32[4,128,256]{2,1,0:T(8,128)S(1)}, f32[4,128,256]{2,1,0:T(8,128)S(1)}, u32[]{:S(2)}, u32[]{:S(2)}) collective-permute-start(f32[4,128,256]{2,1,0:T(8,128)S(1)} %get-tuple-element.12), channel_id=1, source_target_pairs={{0,1},{1,0},{2,3},{3,2},{4,5},{5,4},{6,7},{7,6},{8,9},{9,8},{10,11... | collective-permute-start | bytes 1572872 | tf_op jit(solution)/shard_map/ppermute | solution.py:236
  6.0 6.1 %copy-start.2 = (f32[2048]{0:T(1024)S(1)}, f32[2048]{0:T(1024)}, u32[]{:S(2)}) copy-start(f32[2048]{0:T(1024)} %param.22) | copy-start | bytes 24580
  6.0 6.1 %copy-start.3 = (f32[2048]{0:T(1024)S(1)}, f32[2048]{0:T(1024)}, u32[]{:S(2)}) copy-start(f32[2048]{0:T(1024)} %param.23) | copy-start | bytes 24580
  6.1 9.0 %collective-permute-start.1 = (f32[128,256]{1,0:T(8,128)S(1)}, f32[128,256]{1,0:T(8,128)S(1)}, u32[]{:S(2)}, u32[]{:S(2)}) collective-permute-start(f32[128,256]{1,0:T(8,128)S(1)} %get-tuple-element.20), channel_id=1, source_target_pairs={{0,6},{1,7},{2,0},{3,1},{4,2},{5,3},{6,4},{7,5},{8,14},{9,15},{10,... | collective-permute-start | bytes 393224 | tf_op jit(solution)/shard_map/ppermute | solution.py:251
  11.1 11.7 %collective-permute-start.2 = (f32[128,256]{1,0:T(8,128)S(1)}, f32[128,256]{1,0:T(8,128)S(1)}, u32[]{:S(2)}, u32[]{:S(2)}) collective-permute-start(f32[128,256]{1,0:T(8,128)S(1)} %get-tuple-element.19), channel_id=1, source_target_pairs={{0,4},{1,5},{2,6},{3,7},{4,0},{5,1},{6,2},{7,3},{8,12},{9,13},{10,... | collective-permute-start | bytes 393224 | tf_op jit(solution)/shard_map/ppermute | solution.py:251
  11.1 11.7 %collective-permute-start.3 = (f32[128,256]{1,0:T(8,128)S(1)}, f32[128,256]{1,0:T(8,128)S(1)}, u32[]{:S(2)}, u32[]{:S(2)}) collective-permute-start(f32[128,256]{1,0:T(8,128)S(1)} %get-tuple-element.18), channel_id=1, source_target_pairs={{0,2},{1,3},{2,4},{3,5},{4,6},{5,7},{6,0},{7,1},{8,10},{9,11},{10,... | collective-permute-start | bytes 393224 | tf_op jit(solution)/shard_map/ppermute | solution.py:251
  12.1 0.7 %copy-start.1 = (f32[2048]{0:T(1024)S(1)}, f32[2048]{0:T(1024)}, u32[]{:S(2)}) copy-start(f32[2048]{0:T(1024)} %param.21) | copy-start | bytes 24580
  12.1 0.7 %copy-start = (f32[2048]{0:T(1024)S(1)}, f32[2048]{0:T(1024)}, u32[]{:S(2)}) copy-start(f32[2048]{0:T(1024)} %param.20) | copy-start | bytes 24580
  23.0 4.3 %collective-permute-start.4 = (f32[64,256]{1,0:T(8,128)S(1)}, f32[64,256]{1,0:T(8,128)S(1)}, u32[]{:S(2)}, u32[]{:S(2)}) collective-permute-start(f32[64,256]{1,0:T(8,128)S(1)} %get-tuple-element.15), channel_id=1, source_target_pairs={{0,8},{8,0},{1,9},{9,1},{2,10},{10,2},{3,11},{11,3},{4,12},{12,4},... | collective-permute-start | bytes 196616 | tf_op jit(solution)/shard_map/ppermute | solution.py:265
  28.0 1.2 %collective-permute-start.5 = (f32[64]{0:T(128)S(1)}, f32[64]{0:T(128)S(1)}, u32[]{:S(2)}, u32[]{:S(2)}) collective-permute-start(f32[64]{0:T(128)S(1)} %bitcast.23), channel_id=1, source_target_pairs={{0,1},{1,0},{2,3},{3,2},{4,5},{5,4},{6,7},{7,6},{8,9},{9,8},{10,11... | collective-permute-start | bytes 776 | tf_op jit(solution)/shard_map/ppermute | solution.py:282
  29.2 3.6 %collective-permute-start.6 = (f32[64]{0:T(128)S(1)}, f32[64]{0:T(128)S(1)}, u32[]{:S(2)}, u32[]{:S(2)}) collective-permute-start(f32[64]{0:T(128)S(1)} %bitcast_add_fusion), channel_id=1, source_target_pairs={{0,2},{1,3},{2,0},{3,1},{4,6},{5,7},{6,4},{7,5},{8,10},{9,11},{10,... | collective-permute-start | bytes 776 | tf_op jit(solution)/shard_map/ppermute | solution.py:282
  32.8 4.5 %collective-permute-start.7 = (f32[64]{0:T(128)S(1)}, f32[64]{0:T(128)S(1)}, u32[]{:S(2)}, u32[]{:S(2)}) collective-permute-start(f32[64]{0:T(128)S(1)} %add.38), channel_id=1, source_target_pairs={{0,4},{1,5},{2,6},{3,7},{4,0},{5,1},{6,2},{7,3},{8,12},{9,13},{10,... | collective-permute-start | bytes 776 | tf_op jit(solution)/shard_map/ppermute | solution.py:282

commit v2 on v1

--- a/solution.py
+++ b/solution.py
@@ -11,6 +11,7 @@
 LANES = 128
 SUBLANES = 8
 CORES = 2
+HYBRID = False
 
 f32, bf16, i32 = jnp.float32, jnp.bfloat16, jnp.int32
 HBM = pl.BlockSpec(memory_space=pltpu.HBM)
@@ -54,6 +55,12 @@
         (((1,), (1,)), ((), ())),
         preferred_element_type=f32,
     )
+
+
+def chip_at(chip, k, chips):
+    if chips & (chips - 1) == 0:
+        return chip ^ k
+    return lax.rem(chip + k, chips)
 
 
 def damage_kernel(
@@ -128,7 +135,7 @@
     chip, core = me // CORES, lax.rem(me, CORES)
     loss = loss_ref[...]
     for k in range(chips):
-        owner = lax.rem(chip + k, chips) * CORES + (1 - core)
+        owner = chip_at(chip, k, chips) * CORES + (1 - core)
         send_ref[k] = block_totals(contract_s, loss, owner * share, share)
 
 
@@ -138,20 +145,28 @@
     chip, core = me // CORES, lax.rem(me, CORES)
     loss = loss_ref[...]
     for k in range(chips):
-        owner = lax.rem(chip + k, chips) * CORES + core
+        owner = chip_at(chip, k, chips) * CORES + core
         out_ref[k] = block_totals(contract_s, loss, owner * share, share)
 
 
-def year_kernel(count, *refs):
+def year_kernel(starts, *refs):
+    count = len(starts)
     ins, (terms_ref, year_ref), outs = (
         refs[:count], refs[count : count + 2], refs[count + 2 :]
     )
-    total = ins[0][...]
-    for ref in ins[1:]:
-        total = total + ref[...]
+    events = ins[0].shape[0]
+    bounds = sorted(set(starts) | {events})
+    rows = []
+    for low, high in zip(bounds, bounds[1:]):
+        inside = [
+            ref[low - start : high - start, :]
+            for start, ref in zip(starts, ins)
+            if start <= low and start + ref.shape[0] >= high
+        ]
+        rows.append(functools.reduce(jnp.add, inside))
+    total = jnp.concatenate(rows, axis=0)
     occurrence = jnp.minimum(jnp.maximum(total - terms_ref[0:1, :], 0.0), terms_ref[1:2, :])
     evs = len(outs)
-    events = total.shape[0]
     ev = lax.axis_index("ev")
     for m, out in enumerate(outs):
         first = lax.rem(ev + m, evs) * YR_DEV
@@ -162,19 +177,24 @@
         )
 
 
-def annual_kernel(count, *refs):
-    ins, (terms_ref, annual_ref, part_ref) = refs[:count], refs[count:]
-    yearly = ins[0][...]
-    for ref in ins[1:]:
-        yearly = yearly + ref[...]
-    annual = jnp.minimum(jnp.maximum(yearly - terms_ref[2:3, :], 0.0), terms_ref[3:4, :])
-    annual_ref[...] = annual
-    ones = jnp.ones((SUBLANES, annual.shape[1]), f32)
+def annual_of(ins, terms_ref):
+    yearly = functools.reduce(jnp.add, [ref[...] for ref in ins])
+    return jnp.minimum(jnp.maximum(yearly - terms_ref[2:3, :], 0.0), terms_ref[3:4, :])
+
+
+def part_kernel(*refs):
+    *ins, terms_ref, part_ref = refs
+    annual = annual_of(ins, terms_ref)
     part = lax.dot_general(
-        ones, annual, (((1,), (1,)), ((), ())),
+        jnp.ones((SUBLANES, annual.shape[1]), f32), annual, (((1,), (1,)), ((), ())),
         precision=lax.Precision.HIGHEST, preferred_element_type=f32,
     )
     part_ref[...] = part[0:1, :]
+
+
+def annual_kernel(*refs):
+    *ins, terms_ref, annual_ref = refs
+    annual_ref[...] = annual_of(ins, terms_ref)
 
 
 def params(mib):
@@ -183,6 +203,60 @@
 
 def rotate(size, k):
     return [(i, (i + k) % size) for i in range(size)]
+
+
+def z_pairs(size, offset, only=None):
+    chips = size // CORES
+    return [
+        (
+            chip * CORES + core,
+            ((chip ^ offset) if chips & (chips - 1) == 0 else (chip + offset) % chips) * CORES
+            + core,
+        )
+        for chip in (range(chips) if only is None else only)
+        for core in range(CORES)
+    ]
+
+
+def exchange(own, got):
+    size = lax.axis_size("loc")
+    chips, events, _ = own.shape
+
+    def part(k, rows):
+        return own[k, rows] + got[k, rows]
+
+    every = slice(0, events)
+    if not (HYBRID and chips == 4 and events % (2 * SUBLANES) == 0):
+        return [
+            (0, lax.ppermute(part(k, every), "loc", z_pairs(size, k)))
+            for k in range(chips - 1, 0, -1)
+        ]
+    ahead, rest = slice(0, events // 2), slice(events // 2, events)
+    far, mid = part(2, ahead), part(3, ahead)
+    relay = lax.ppermute(jnp.concatenate([mid, far]), "loc", z_pairs(size, 1, (0, 3)))
+    late3 = lax.ppermute(part(3, rest), "loc", z_pairs(size, 3))
+    late2 = lax.ppermute(part(2, rest), "loc", z_pairs(size, 2))
+    near = lax.ppermute(part(1, every), "loc", z_pairs(size, 1))
+    half = events // 2
+    mid = lax.ppermute(mid + relay[half:], "loc", z_pairs(size, 3, (1, 2)))
+    far = lax.ppermute(far + relay[:half], "loc", z_pairs(size, 2, (1, 2)))
+    return [(0, near), (half, late3), (half, late2), (0, mid), (0, far)]
+
+
+def mean_over_loc(part):
+    size = lax.axis_size("loc")
+    if size & (size - 1) or size < 2 * CORES:
+        return lax.psum(part, "loc")
+
+    def swap(x, k):
+        return lax.ppermute(x, "loc", [(i, i ^ k) for i in range(size)])
+
+    total = (part + swap(part, 1)) + (swap(part, 2) + swap(part, 3))
+    step = 4
+    while step < size:
+        total = total + swap(total, step)
+        step *= 2
+    return total
 
 
 def local(
@@ -243,18 +317,13 @@
         cost_estimate=pl.CostEstimate(flops=10**9, bytes_accessed=2 << 20, transcendentals=0),
         name="own_part",
     )(contract_v, loss)
-    blocks = [own[0], got[0]]
-    for k in range(chips - 1, 0, -1):
-        pairs = [
-            (i, ((i // CORES + k) % chips) * CORES + i % CORES) for i in range(loc_count)
-        ]
-        blocks.append(lax.ppermute(own[k] + got[k], "loc", pairs))
+    starts, blocks = zip(*([(0, own[0]), (0, got[0])] + exchange(own, got)))
     first = lax.axis_index("loc") * share
     terms = lax.dynamic_slice(
         jnp.stack([occ_retention, occ_limit, agg_retention, agg_limit]), (0, first), (4, share)
     )
     yearly = pl.pallas_call(
-        functools.partial(year_kernel, len(blocks)),
+        functools.partial(year_kernel, starts),
         out_shape=tuple(jax.ShapeDtypeStruct((YR_DEV, share), f32) for _ in range(evs)),
         in_specs=[VMEM] * (len(blocks) + 2),
         out_specs=tuple(VMEM for _ in range(evs)),
@@ -264,25 +333,24 @@
     sums = [yearly[0]] + [
         lax.ppermute(yearly[m], "ev", rotate(evs, m)) for m in range(1, evs)
     ]
-    annual, part = pl.pallas_call(
-        functools.partial(annual_kernel, len(sums)),
-        out_shape=(
-            jax.ShapeDtypeStruct((YR_DEV, share), f32),
-            jax.ShapeDtypeStruct((1, YR_DEV), f32),
-        ),
+    part = pl.pallas_call(
+        part_kernel,
+        out_shape=jax.ShapeDtypeStruct((1, YR_DEV), f32),
         in_specs=[VMEM] * (len(sums) + 1),
-        out_specs=(VMEM, VMEM),
-        compiler_params=params(16),
+        out_specs=VMEM,
+        compiler_params=params(8),
+        name="mean_part",
+    )(*sums, terms)
+    mean = mean_over_loc(part.reshape(YR_DEV))
+    annual = pl.pallas_call(
+        annual_kernel,
+        out_shape=jax.ShapeDtypeStruct((YR_DEV, share), f32),
+        in_specs=[VMEM] * (len(sums) + 1),
+        out_specs=VMEM,
+        compiler_params=params(8),
+        cost_estimate=pl.CostEstimate(flops=10**6, bytes_accessed=1 << 20, transcendentals=0),
         name="annual",
     )(*sums, terms)
-    mean = part.reshape(YR_DEV)
-    if loc_count & (loc_count - 1) == 0:
-        step = 1
-        while step < loc_count:
-            mean = mean + lax.ppermute(mean, "loc", [(i, i ^ step) for i in range(loc_count)])
-            step *= 2
-    else:
-        mean = lax.psum(mean, "loc")
     return annual.T, mean / contract_count
 
 

time: 37.9 us -> 36.1 us (0.953)
  waiting for transfers between devices: 19.5 us -> 16.5 us
  starting transfers between devices: 11.2 us -> 12.2 us
    ppermute x6 -> x7, waiting for transfers between devices: 16 us -> 13.1 us  [the longest x3 9.93 us: exchange(): lax.ppermute(part(k, every), 'loc', z_pairs(size, k))]
    ppermute x6 -> x7, starting transfers between devices: 9.09 us -> 10 us  [the longest x3 5.67 us: exchange(): lax.ppermute(part(k, every), 'loc', z_pairs(size, k))]
    pallas_call x2 -> x3, Pallas kernels: 0.94 us -> 1.08 us  [the longest x1 0.64 us: local(): pl.pallas_call(annual_kernel, out_shape=jax.ShapeDtypeStruct((YR_DEV, sha...]
  transfers between devices with their start and end apart: 8 -> 9, of which waited for: 7 -> 6; matrix products, arithmetic and copies ran while one was open for 0% -> 0% of each run, Pallas kernels for 2% -> 4%
where the time goes in v2:
time: 36.1 us; the launch traced here: 35.9 us
  waiting for transfers between devices  16.5 us (46%)
  starting transfers between devices  12.2 us (34%)
  Pallas kernels  5.15 us (14%)
  local copies, waits for them, and re-layouts  0.71 us (2%)
  between operations  0.69 us (2%)
  other arithmetic  0.67 us (2%)
    ppermute x3, waiting for transfers between devices, exchange(): lax.ppermute(part(k, every), 'loc', z_pairs(size, k))  9.93 us
    ppermute x3, starting transfers between devices, exchange(): lax.ppermute(part(k, every), 'loc', z_pairs(size, k))  5.67 us
    ppermute x4, starting transfers between devices, swap(): return lax.ppermute(x, 'loc', [(i, i ^ k) for i in range(size)])  4.37 us
    pallas_call x1, Pallas kernels, local(): pl.pallas_call(functools.partial(damage_kernel, share, parts), out_shape=...  3.24 us
    ppermute x4, waiting for transfers between devices, swap(): return lax.ppermute(x, 'loc', [(i, i ^ k) for i in range(size)])  3.12 us
    ppermute x1, waiting for transfers between devices, local(): lax.ppermute(yearly[m], 'ev', rotate(evs, m))  2.78 us
    ppermute x1, starting transfers between devices, local(): lax.ppermute(yearly[m], 'ev', rotate(evs, m))  1.55 us
    pallas_call x1, Pallas kernels, local(): pl.pallas_call(functools.partial(own_kernel, share), out_shape=jax.ShapeD...  0.83 us
  transfers between devices with their start and end apart: 9, of which 6 were waited for; matrix products, arithmetic and copies ran while one was open for 0% of the time, Pallas kernels for 4%

profile of v2, /device:TPU:0, one launch (start us, length us, event | category | flops | bytes accessed | tf_op | source)
XLA Modules:
  0.0 35.9 jit_solution(2718399539884348873)
XLA Ops:
  0.6 3.2 %damage.1 = (f32[4,128,256]{2,1,0:T(8,128)S(1)}, bf16[128,1024]{1,0:T(8,128)(2,1)S(1)}, s32[8,128]{1,0:T(8,128)S(1)}, s32[1,128]{1,0:T(1,128)S(1)}) custom-call(s32[128,1024]{1,0:T(8,128)} %bins_h.1, bf16[128,1024]{1,0:T(8,128)(2,1)} %frac_h.1, s32[8,128]{1,0:T(8,128)} %bitcast.32, s32[8,128]{1,0:T(8,128)} %bitcast.33, f32[8,128]{1,0:T(8,128)} %bitcast.34, ...), custom_call_target="tpu_custom_call" | custom-call | flops 1000000000 | bytes 2097152 | tf_op jit(solution)/shard_map/damage/pallas_call | solution.py:276
  3.9 0.6 %collective-permute-start = (f32[4,128,256]{2,1,0:T(8,128)S(1)}, f32[4,128,256]{2,1,0:T(8,128)S(1)}, u32[]{:S(2)}, u32[]{:S(2)}) collective-permute-start(f32[4,128,256]{2,1,0:T(8,128)S(1)} %get-tuple-element.10), channel_id=1, source_target_pairs={{0,1},{1,0},{2,3},{3,2},{4,5},{5,4},{6,7},{7,6},{8,9},{9,8},{10,11... | collective-permute-start | bytes 1572872 | tf_op jit(solution)/shard_map/ppermute | solution.py:310
  4.4 0.8 %own_part.1 = f32[4,128,256]{2,1,0:T(8,128)S(1)} custom-call(s32[8,128]{1,0:T(8,128)S(1)} %get-tuple-element.8.contract_s, bf16[128,1024]{1,0:T(8,128)(2,1)S(1)} %get-tuple-element.9.loss_ref), custom_call_target="tpu_custom_call" | custom-call | flops 1000000000 | bytes 2097152 | tf_op jit(solution)/shard_map/own_part/pallas_call | solution.py:311
  5.3 0.7 %collective-permute-done = f32[4,128,256]{2,1,0:T(8,128)S(1)} collective-permute-done((f32[4,128,256]{2,1,0:T(8,128)S(1)}, f32[4,128,256]{2,1,0:T(8,128)S(1)}, u32[]{:S(2)}, u32[]{:S(2)}) %collective-permute-start) | collective-permute-done | bytes 524320 | tf_op jit(solution)/shard_map/ppermute | solution.py:310
  6.0 0.0 copy-start.2
  6.0 0.0 copy-start.3
  6.0 0.1 fusion
  6.1 5.0 %collective-permute-start.1 = (f32[128,256]{1,0:T(8,128)S(1)}, f32[128,256]{1,0:T(8,128)S(1)}, u32[]{:S(2)}, u32[]{:S(2)}) collective-permute-start(f32[128,256]{1,0:T(8,128)S(1)} %get-tuple-element.16), channel_id=1, source_target_pairs={{0,6},{1,7},{2,4},{3,5},{4,2},{5,3},{6,0},{7,1},{8,14},{9,15},{10,... | collective-permute-start | bytes 393224 | tf_op jit(solution)/shard_map/ppermute | solution.py:231
  11.1 0.0 collective-permute-start.2
  11.1 0.6 %collective-permute-start.3 = (f32[128,256]{1,0:T(8,128)S(1)}, f32[128,256]{1,0:T(8,128)S(1)}, u32[]{:S(2)}, u32[]{:S(2)}) collective-permute-start(f32[128,256]{1,0:T(8,128)S(1)} %get-tuple-element.14), channel_id=1, source_target_pairs={{0,2},{1,3},{2,0},{3,1},{4,6},{5,7},{6,4},{7,5},{8,10},{9,11},{10,... | collective-permute-start | bytes 393224 | tf_op jit(solution)/shard_map/ppermute | solution.py:231
  11.7 0.0 copy-start.1
  11.7 0.0 copy-start
  11.7 0.0 copy-done.2
  11.7 0.0 copy-done.3
  11.7 0.7 %copy-done.1 = f32[2048]{0:T(1024)S(1)} copy-done((f32[2048]{0:T(1024)S(1)}, f32[2048]{0:T(1024)}, u32[]{:S(2)}) %copy-start.1) | copy-done | bytes 8216
  12.4 0.0 copy-done
  12.4 0.1 fusion.5.refs_5_.refs_2_
  12.5 3.0 %collective-permute-done.1.refs_2_ = f32[128,256]{1,0:T(8,128)S(1)} collective-permute-done((f32[128,256]{1,0:T(8,128)S(1)}, f32[128,256]{1,0:T(8,128)S(1)}, u32[]{:S(2)}, u32[]{:S(2)}) %collective-permute-start.1) | collective-permute-done | bytes 131104 | tf_op jit(solution)/shard_map/ppermute | solution.py:231
  15.5 6.9 %collective-permute-done.2.refs_3_ = f32[128,256]{1,0:T(8,128)S(1)} collective-permute-done((f32[128,256]{1,0:T(8,128)S(1)}, f32[128,256]{1,0:T(8,128)S(1)}, u32[]{:S(2)}, u32[]{:S(2)}) %collective-permute-start.2) | collective-permute-done | bytes 131104 | tf_op jit(solution)/shard_map/ppermute | solution.py:231
  22.5 0.0 collective-permute-done.3.refs_4_
  22.5 0.3 years.1
  22.8 1.6 %collective-permute-start.4 = (f32[64,256]{1,0:T(8,128)S(1)}, f32[64,256]{1,0:T(8,128)S(1)}, u32[]{:S(2)}, u32[]{:S(2)}) collective-permute-start(f32[64,256]{1,0:T(8,128)S(1)} %get-tuple-element.13), channel_id=1, source_target_pairs={{0,8},{8,0},{1,9},{9,1},{2,10},{10,2},{3,11},{11,3},{4,12},{12,4},... | collective-permute-start | bytes 196616 | tf_op jit(solution)/shard_map/ppermute | solution.py:334
  24.3 2.8 %collective-permute-done.4.refs_1_ = f32[64,256]{1,0:T(8,128)S(1)} collective-permute-done((f32[64,256]{1,0:T(8,128)S(1)}, f32[64,256]{1,0:T(8,128)S(1)}, u32[]{:S(2)}, u32[]{:S(2)}) %collective-permute-start.4) | collective-permute-done | bytes 65568 | tf_op jit(solution)/shard_map/ppermute | solution.py:334
  27.1 0.2 mean_part.1
  27.2 0.0 collective-permute-start.5
  27.2 0.0 collective-permute-start.6
  27.3 1.8 %collective-permute-start.7 = (f32[64]{0:T(128)S(1)}, f32[64]{0:T(128)S(1)}, u32[]{:S(2)}, u32[]{:S(2)}) collective-permute-start(f32[64]{0:T(128)S(1)} %bitcast.25), channel_id=1, source_target_pairs={{0,3},{1,2},{2,1},{3,0},{4,7},{5,6},{6,5},{7,4},{8,11},{9,10},{10,... | collective-permute-start | bytes 776 | tf_op jit(solution)/shard_map/ppermute | solution.py:252
  29.1 0.0 collective-permute-done.5
  29.1 1.7 %collective-permute-done.6 = f32[64]{0:T(128)S(1)} collective-permute-done((f32[64]{0:T(128)S(1)}, f32[64]{0:T(128)S(1)}, u32[]{:S(2)}, u32[]{:S(2)}) %collective-permute-start.6) | collective-permute-done | bytes 288 | tf_op jit(solution)/shard_map/ppermute | solution.py:252
  30.8 0.0 collective-permute-done.7
  30.9 2.5 %collective-permute-start.8 = (f32[64]{0:T(128)S(1)}, f32[64]{0:T(128)S(1)}, u32[]{:S(2)}, u32[]{:S(2)}) collective-permute-start(f32[64]{0:T(128)S(1)} %add_add_fusion), channel_id=1, source_target_pairs={{0,4},{1,5},{2,6},{3,7},{4,0},{5,1},{6,2},{7,3},{8,12},{9,13},{10,... | collective-permute-start | bytes 776 | tf_op jit(solution)/shard_map/ppermute | solution.py:252
  33.3 0.6 %annual.1 = f32[64,256]{1,0:T(8,128)} custom-call(f32[64,256]{1,0:T(8,128)S(1)} %get-tuple-element.12.refs_0_, f32[64,256]{1,0:T(8,128)S(1)} %collective-permute-done.4.refs_1_, f32[4,256]{1,0:T(4,128)S(1)} %fusion.5.refs_5_.refs_2_), custom_call_target="tpu_custom_call" | custom-call | flops 1000000 | bytes 1048576 | tf_op jit(solution)/shard_map/annual/pallas_call | solution.py:345
  34.0 1.4 %collective-permute-done.8 = f32[64]{0:T(128)S(1)} collective-permute-done((f32[64]{0:T(128)S(1)}, f32[64]{0:T(128)S(1)}, u32[]{:S(2)}, u32[]{:S(2)}) %collective-permute-start.8) | collective-permute-done | bytes 288 | tf_op jit(solution)/shard_map/ppermute | solution.py:252
  35.4 0.5 %add_multiply_fusion = f32[64]{0:T(128)} fusion(f32[64]{0:T(128)S(1)} %add_add_fusion, f32[64]{0:T(128)S(1)} %collective-permute-done.8), kind=kLoop, calls=%fused_computation.15 | loop fusion | flops 128 | bytes 768 | tf_op jit(solution)/shard_map/div | solution.py:354
  (1 shorter events, 0.0 us)
Async XLA Ops:
  3.9 2.1 %collective-permute-start = (f32[4,128,256]{2,1,0:T(8,128)S(1)}, f32[4,128,256]{2,1,0:T(8,128)S(1)}, u32[]{:S(2)}, u32[]{:S(2)}) collective-permute-start(f32[4,128,256]{2,1,0:T(8,128)S(1)} %get-tuple-element.10), channel_id=1, source_target_pairs={{0,1},{1,0},{2,3},{3,2},{4,5},{5,4},{6,7},{7,6},{8,9},{9,8},{10,11... | collective-permute-start | bytes 1572872 | tf_op jit(solution)/shard_map/ppermute | solution.py:310
  6.0 5.8 %copy-start.2 = (f32[2048]{0:T(1024)S(1)}, f32[2048]{0:T(1024)}, u32[]{:S(2)}) copy-start(f32[2048]{0:T(1024)} %param.22) | copy-start | bytes 24580
  6.0 5.8 %copy-start.3 = (f32[2048]{0:T(1024)S(1)}, f32[2048]{0:T(1024)}, u32[]{:S(2)}) copy-start(f32[2048]{0:T(1024)} %param.23) | copy-start | bytes 24580
  6.1 9.5 %collective-permute-start.1 = (f32[128,256]{1,0:T(8,128)S(1)}, f32[128,256]{1,0:T(8,128)S(1)}, u32[]{:S(2)}, u32[]{:S(2)}) collective-permute-start(f32[128,256]{1,0:T(8,128)S(1)} %get-tuple-element.16), channel_id=1, source_target_pairs={{0,6},{1,7},{2,4},{3,5},{4,2},{5,3},{6,0},{7,1},{8,14},{9,15},{10,... | collective-permute-start | bytes 393224 | tf_op jit(solution)/shard_map/ppermute | solution.py:231
  11.1 11.4 %collective-permute-start.2 = (f32[128,256]{1,0:T(8,128)S(1)}, f32[128,256]{1,0:T(8,128)S(1)}, u32[]{:S(2)}, u32[]{:S(2)}) collective-permute-start(f32[128,256]{1,0:T(8,128)S(1)} %get-tuple-element.15), channel_id=1, source_target_pairs={{0,4},{1,5},{2,6},{3,7},{4,0},{5,1},{6,2},{7,3},{8,12},{9,13},{10,... | collective-permute-start | bytes 393224 | tf_op jit(solution)/shard_map/ppermute | solution.py:231
  11.1 11.4 %collective-permute-start.3 = (f32[128,256]{1,0:T(8,128)S(1)}, f32[128,256]{1,0:T(8,128)S(1)}, u32[]{:S(2)}, u32[]{:S(2)}) collective-permute-start(f32[128,256]{1,0:T(8,128)S(1)} %get-tuple-element.14), channel_id=1, source_target_pairs={{0,2},{1,3},{2,0},{3,1},{4,6},{5,7},{6,4},{7,5},{8,10},{9,11},{10,... | collective-permute-start | bytes 393224 | tf_op jit(solution)/shard_map/ppermute | solution.py:231
  11.7 0.7 %copy-start.1 = (f32[2048]{0:T(1024)S(1)}, f32[2048]{0:T(1024)}, u32[]{:S(2)}) copy-start(f32[2048]{0:T(1024)} %param.21) | copy-start | bytes 24580
  11.7 0.7 %copy-start = (f32[2048]{0:T(1024)S(1)}, f32[2048]{0:T(1024)}, u32[]{:S(2)}) copy-start(f32[2048]{0:T(1024)} %param.20) | copy-start | bytes 24580
  22.8 4.3 %collective-permute-start.4 = (f32[64,256]{1,0:T(8,128)S(1)}, f32[64,256]{1,0:T(8,128)S(1)}, u32[]{:S(2)}, u32[]{:S(2)}) collective-permute-start(f32[64,256]{1,0:T(8,128)S(1)} %get-tuple-element.13), channel_id=1, source_target_pairs={{0,8},{8,0},{1,9},{9,1},{2,10},{10,2},{3,11},{11,3},{4,12},{12,4},... | collective-permute-start | bytes 196616 | tf_op jit(solution)/shard_map/ppermute | solution.py:334
  27.2 1.9 %collective-permute-start.5 = (f32[64]{0:T(128)S(1)}, f32[64]{0:T(128)S(1)}, u32[]{:S(2)}, u32[]{:S(2)}) collective-permute-start(f32[64]{0:T(128)S(1)} %bitcast.23), channel_id=1, source_target_pairs={{0,1},{1,0},{2,3},{3,2},{4,5},{5,4},{6,7},{7,6},{8,9},{9,8},{10,11... | collective-permute-start | bytes 776 | tf_op jit(solution)/shard_map/ppermute | solution.py:252
  27.2 3.6 %collective-permute-start.6 = (f32[64]{0:T(128)S(1)}, f32[64]{0:T(128)S(1)}, u32[]{:S(2)}, u32[]{:S(2)}) collective-permute-start(f32[64]{0:T(128)S(1)} %bitcast.24), channel_id=1, source_target_pairs={{0,2},{1,3},{2,0},{3,1},{4,6},{5,7},{6,4},{7,5},{8,10},{9,11},{10,... | collective-permute-start | bytes 776 | tf_op jit(solution)/shard_map/ppermute | solution.py:252
  27.3 3.6 %collective-permute-start.7 = (f32[64]{0:T(128)S(1)}, f32[64]{0:T(128)S(1)}, u32[]{:S(2)}, u32[]{:S(2)}) collective-permute-start(f32[64]{0:T(128)S(1)} %bitcast.25), channel_id=1, source_target_pairs={{0,3},{1,2},{2,1},{3,0},{4,7},{5,6},{6,5},{7,4},{8,11},{9,10},{10,... | collective-permute-start | bytes 776 | tf_op jit(solution)/shard_map/ppermute | solution.py:252
  30.9 4.5 %collective-permute-start.8 = (f32[64]{0:T(128)S(1)}, f32[64]{0:T(128)S(1)}, u32[]{:S(2)}, u32[]{:S(2)}) collective-permute-start(f32[64]{0:T(128)S(1)} %add_add_fusion), channel_id=1, source_target_pairs={{0,4},{1,5},{2,6},{3,7},{4,0},{5,1},{6,2},{7,3},{8,12},{9,13},{10,... | collective-permute-start | bytes 776 | tf_op jit(solution)/shard_map/ppermute | solution.py:252
